TPU v7x, 256 devices: a whole 4x4x8 slice. The times are simulated.
256 devices in a mesh: dp: 8 (over x_hi, y), ctx: 32 (over x_lo, z, core).
Axes of the slice: x: 4 (x_hi: 2, x_lo: 2; x = x_hi * 2 + x_lo), y: 4, z: 8, core: 2. Of those that a mesh axis runs over, the one named last changes fastest.
Arguments:
- query: bfloat16 [32768, 512], P(('dp', 'ctx')), may hold values from -6 to 6
- key: bfloat16 [32768, 512], P(('dp', 'ctx')), may hold values from -6 to 6
- value: bfloat16 [32768, 512], P(('dp', 'ctx'))
- gate: bfloat16 [32768, 512], P(('dp', 'ctx')), may hold values from -6 to 6
- out_weight: bfloat16 [512, 1024], replicated, may hold values from -0.25 to 0.25
- items: bfloat16 [1024, 1024], P('ctx'), may hold values from -0.1875 to 0.1875
- cotangent: bfloat16 [32768, 1024], P(('dp', 'ctx')), may hold values from -6 to 6
- user_blocks: int32 [8, 4], P('dp'), may hold values from 1 to 16, 32 in all within a row
- tail_rows: int32 [8, 4], P('dp'), may hold values from 1 to 128
- packing: int32 [8, 32], P('dp'), may hold values from 0 to 31, each once within a row
- cand_ids: int32 [8, 4, 128], P('dp'), may hold values from 0 to 1023
Outputs:
- scores: float32 [32768, 128], P(('dp', 'ctx'))
- grad_query: bfloat16 [32768, 512], P(('dp', 'ctx'))
- grad_key: bfloat16 [32768, 512], P(('dp', 'ctx'))
- grad_value: bfloat16 [32768, 512], P(('dp', 'ctx'))
- grad_gate: bfloat16 [32768, 512], P(('dp', 'ctx'))
- grad_out_weight: float32 [512, 1024], replicated
Inputs may be any that keep to these rules, and one draw needn't show every extreme that they name: `user_blocks`: in each group the 4 counts sum to 32 and the largest is exactly 16. `packing`: each group's row is a permutation of its 32 logical blocks; slots run device by device along ctx. `cand_ids`: rows of the item table.
All inputs are finite; a program needn't handle non-finite values.
Results may differ from a plain program's by a relative error of at most 0.0058.
Values may be sent and summed in bfloat16 or wider, within the bound.
No kernel may reach another device: no remote copies, remote signals or barrier semaphores. Data moves between devices by JAX's collectives and lax.ppermute only.
A program may use at most 128 MiB of HBM per device.

v0:
```python
import jax
import jax.numpy as jnp
from jax import lax
from jax.sharding import PartitionSpec as P

HEADS = 4
HEAD_DIM = 128
BLOCK = 128
norm_eps = 1e-05


def row_facts(blocks, tails, layout, offset, length):
    row_index = offset + jnp.arange(length, dtype=jnp.int32)
    slot_index = row_index // BLOCK
    within = row_index % BLOCK
    user_ends = jnp.cumsum(blocks)
    user_starts = user_ends - blocks
    user_rows = (blocks - 1) * BLOCK + tails
    slot_match = slot_index[:, None] == jnp.arange(layout.shape[0], dtype=jnp.int32)[None, :]
    logical = jnp.sum(jnp.where(slot_match, layout[None, :], 0), axis=1)
    user_of = jnp.sum((logical[:, None] >= user_ends[None, :]).astype(jnp.int32), axis=1)
    user_match = user_of[:, None] == jnp.arange(blocks.shape[0], dtype=jnp.int32)[None, :]
    first_row = jnp.sum(jnp.where(user_match, user_starts[None, :], 0), axis=1) * BLOCK
    row_limit = jnp.sum(jnp.where(user_match, user_rows[None, :], 0), axis=1)
    position = logical * BLOCK + within
    is_valid = position - first_row < row_limit
    return (user_of, position, is_valid)


def pair_mask(query_facts, key_facts):
    same_user = query_facts[0][:, None] == key_facts[0][None, :]
    earlier = key_facts[1][None, :] <= query_facts[1][:, None]
    both_valid = query_facts[2][:, None] & key_facts[2][None, :]
    return same_user & earlier & both_valid


def silu_slope(values):
    sigma = jax.nn.sigmoid(values)
    return sigma * (1.0 + values * (1.0 - sigma))


def split_heads(array):
    return array.reshape(array.shape[0], HEADS, HEAD_DIM)


def blockwise(step, running, pieces):
    length = pieces[0].shape[0]
    stride = 512
    count = length // stride
    stacked = tuple((piece.reshape((count, stride) + piece.shape[1:]) for piece in pieces))
    offsets = jnp.arange(count, dtype=jnp.int32) * stride

    def advance(state, inputs):
        return (step(state, inputs[0], inputs[1]), None)

    result, unused = lax.scan(advance, running, (stacked, offsets))
    return result


def body(
    query, key, value, gate, out_weight, items, cotangent, user_blocks, tail_rows, packing, cand_ids
):
    local_rows = query.shape[0]
    attn_width = query.shape[1]
    score_scale = HEAD_DIM ** (-0.5)
    blocks = user_blocks[0]
    tails = tail_rows[0]
    layout = packing[0]
    candidates = cand_ids[0]
    ctx_index = lax.axis_index("ctx")
    local_facts = row_facts(blocks, tails, layout, ctx_index * local_rows, local_rows)
    query_heads = split_heads(query)
    key_heads = split_heads(key)
    value_heads = split_heads(value)
    zeros_heads = jnp.zeros((local_rows, HEADS, HEAD_DIM), jnp.float32)

    def forward_step(running, pieces, offset):
        key_piece = split_heads(pieces[0])
        value_piece = split_heads(pieces[1])
        allowed = pair_mask(
            local_facts, row_facts(blocks, tails, layout, offset, key_piece.shape[0])
        )
        logits = (
            jnp.einsum("qhd,khd->hqk", query_heads, key_piece, preferred_element_type=jnp.float32)
            * score_scale
        )
        weights = (jax.nn.silu(logits) * allowed[None]).astype(jnp.bfloat16)
        return running + jnp.einsum(
            "hqk,khd->qhd", weights, value_piece, preferred_element_type=jnp.float32
        )

    attended = blockwise(
        forward_step,
        zeros_heads,
        (
            lax.all_gather(key, "ctx", axis=0, tiled=True),
            lax.all_gather(value, "ctx", axis=0, tiled=True),
        ),
    )
    attended = attended.reshape(local_rows, attn_width)
    row_mean = jnp.mean(attended, axis=1, keepdims=True)
    centered = attended - row_mean
    inv_std = lax.rsqrt(jnp.mean(centered * centered, axis=1, keepdims=True) + norm_eps)
    normed = centered * inv_std
    valid_col = local_facts[2].astype(jnp.float32)[:, None]
    gate_float = gate.astype(jnp.float32)
    mixed = (valid_col * normed * gate_float).astype(jnp.bfloat16)
    output = jnp.dot(mixed, out_weight, preferred_element_type=jnp.float32).astype(jnp.bfloat16)
    all_scores = lax.dot_general(
        output,
        lax.all_gather(items, "ctx", axis=0, tiled=True),
        (((1,), (1,)), ((), ())),
        preferred_element_type=jnp.float32,
    )
    user_match = (
        local_facts[0][:, None] == jnp.arange(candidates.shape[0], dtype=jnp.int32)[None, :]
    )
    picked = jnp.sum(jnp.where(user_match[:, :, None], candidates[None, :, :], 0), axis=1)
    scores = jnp.take_along_axis(all_scores, picked, axis=1)
    weight_local = lax.dot_general(
        mixed, cotangent, (((0,), (0,)), ((), ())), preferred_element_type=jnp.float32
    )
    grad_out_weight = lax.psum(weight_local, ("dp", "ctx"))
    grad_mixed = lax.dot_general(
        cotangent, out_weight, (((1,), (1,)), ((), ())), preferred_element_type=jnp.float32
    )
    grad_gate = (grad_mixed * valid_col * normed).astype(jnp.bfloat16)
    grad_normed = grad_mixed * valid_col * gate_float
    grad_attended = (
        (
            grad_normed
            - jnp.mean(grad_normed, axis=1, keepdims=True)
            - normed * jnp.mean(grad_normed * normed, axis=1, keepdims=True)
        )
        * inv_std
    ).astype(jnp.bfloat16)
    grad_heads = split_heads(grad_attended)

    def query_step(running, pieces, offset):
        key_piece = split_heads(pieces[0])
        value_piece = split_heads(pieces[1])
        allowed = pair_mask(
            local_facts, row_facts(blocks, tails, layout, offset, key_piece.shape[0])
        )
        logits = (
            jnp.einsum("qhd,khd->hqk", query_heads, key_piece, preferred_element_type=jnp.float32)
            * score_scale
        )
        slopes = jnp.einsum(
            "qhd,khd->hqk", grad_heads, value_piece, preferred_element_type=jnp.float32
        )
        grad_logits = (slopes * allowed[None] * silu_slope(logits)).astype(jnp.bfloat16)
        return running + jnp.einsum(
            "hqk,khd->qhd", grad_logits, key_piece, preferred_element_type=jnp.float32
        )

    query_sum = blockwise(
        query_step,
        zeros_heads,
        (
            lax.all_gather(key, "ctx", axis=0, tiled=True),
            lax.all_gather(value, "ctx", axis=0, tiled=True),
        ),
    )

    def key_step(running, pieces, offset):
        query_piece = split_heads(pieces[0])
        grad_piece = split_heads(pieces[1])
        allowed = pair_mask(
            row_facts(blocks, tails, layout, offset, query_piece.shape[0]), local_facts
        )
        logits = (
            jnp.einsum("qhd,khd->hqk", query_piece, key_heads, preferred_element_type=jnp.float32)
            * score_scale
        )
        weights = (jax.nn.silu(logits) * allowed[None]).astype(jnp.bfloat16)
        slopes = jnp.einsum(
            "qhd,khd->hqk", grad_piece, value_heads, preferred_element_type=jnp.float32
        )
        grad_logits = (slopes * allowed[None] * silu_slope(logits)).astype(jnp.bfloat16)
        key_sum = running[0] + jnp.einsum(
            "hqk,qhd->khd", grad_logits, query_piece, preferred_element_type=jnp.float32
        )
        value_sum = running[1] + jnp.einsum(
            "hqk,qhd->khd", weights, grad_piece, preferred_element_type=jnp.float32
        )
        return (key_sum, value_sum)

    key_sum, value_sum = blockwise(
        key_step,
        (zeros_heads, zeros_heads),
        (
            lax.all_gather(query, "ctx", axis=0, tiled=True),
            lax.all_gather(grad_attended, "ctx", axis=0, tiled=True),
        ),
    )
    grad_query = (query_sum.reshape(local_rows, attn_width) * score_scale).astype(jnp.bfloat16)
    grad_key = (key_sum.reshape(local_rows, attn_width) * score_scale).astype(jnp.bfloat16)
    grad_value = value_sum.reshape(local_rows, attn_width).astype(jnp.bfloat16)
    return (scores, grad_query, grad_key, grad_value, grad_gate, grad_out_weight)


def solution(mesh):
    in_specs = (
        P(("dp", "ctx"), None),
        P(("dp", "ctx"), None),
        P(("dp", "ctx"), None),
        P(("dp", "ctx"), None),
        P(),
        P("ctx", None),
        P(("dp", "ctx"), None),
        P("dp", None),
        P("dp", None),
        P("dp", None),
        P("dp", None, None),
    )
    out_specs = (
        P(("dp", "ctx"), None),
        P(("dp", "ctx"), None),
        P(("dp", "ctx"), None),
        P(("dp", "ctx"), None),
        P(("dp", "ctx"), None),
        P(),
    )
    return jax.shard_map(body, mesh=mesh, in_specs=in_specs, out_specs=out_specs, check_vma=False)
```

profile of v0, /device:TPU:2, one launch (start us, length us, event | category | flops | bytes accessed | tf_op | source)
XLA Modules:
  0.0 709.0 jit_solution(13533291843244963831)
XLA Ops:
  20.4 58.6 %all-gather.6.cloned.1.call-done = bf16[4096,512]{1,0:T(8,128)(2,1)} async-done(((bf16[128,512]{1,0:T(8,128)(2,1)}), bf16[4096,512]{1,0:T(8,128)(2,1)}) %all-gather.6.cloned.1.call-update) | async-done | bytes 4194320 | tf_op jit(solution)/shard_map/all_gather | solution.py:97
  79.1 6.5 copy.119
  85.6 61.9 %all-gather.8.cloned.1.call-done = bf16[4096,512]{1,0:T(8,128)(2,1)} async-done(((bf16[128,512]{1,0:T(8,128)(2,1)}), bf16[4096,512]{1,0:T(8,128)(2,1)}) %all-gather.8.cloned.1.call-update) | async-done | bytes 4194320 | tf_op jit(solution)/shard_map/all_gather | solution.py:96
  147.4 6.5 copy.120
  153.9 63.8 %while.44 = (s32[]{:T(128)}, f32[128,4,128]{0,2,1:T(8,128)S(1)}, bf16[8,512,512]{1,2,0:T(8,128)(2,1)}, bf16[8,512,512]{1,2,0:T(8,128)(2,1)}, bf16[128,4,128]{2,0...) while((s32[]{:T(128)}, f32[128,4,128]{0,2,1:T(8,128)S(1)}, ...), condition=%wide.region_11.12_spmd.clone, body=%wide.region_6.11_spmd.clone.sunk | while | flops 136657424 | bytes 4356639 | solution.py:56
  220.3 80.3 %while.45 = (s32[]{:T(128)}, f32[128,4,128]{0,2,1:T(8,128)}, bf16[8,512,512]{1,2,0:T(8,128)(2,1)}, bf16[8,512,512]{1,2,0:T(8,128)(2,1)}, bf16[128,4,128]{2,0,1:T...) while((s32[]{:T(128)}, f32[128,4,128]{0,2,1:T(8,128)}, ...), condition=%wide.region_21.22_spmd.clone, body=%wide.region_16.21_spmd.clone.sunk | while | flops 204814864 | bytes 7109159 | solution.py:56
  237.8 2.5 fusion.118
  247.9 2.5 fusion.118
  258.0 2.5 fusion.118
  268.0 2.5 fusion.118
  278.1 2.5 fusion.118
  298.1 2.5 fusion.118
  302.4 2.7 fusion.53
  305.1 129.5 %gather_fusion = f32[16384]{0:T(1024)S(1)} fusion(f32[128,1024]{1,0:T(8,128)S(1)} %fusion.53, s32[16384]{0:T(1024)S(1)} %fusion.59), kind=kCustom, calls=%fused_computation | custom fusion | bytes 262144 | tf_op jit(solution)/shard_map/jit(take_along_axis)/gather | solution.py:119
  437.1 92.8 %while.46 = (s32[]{:T(128)}, f32[128,4,128]{0,2,1:T(8,128)}, f32[128,4,128]{0,2,1:T(8,128)}, bf16[8,512,512]{2,1,0:T(8,128)(2,1)}, bf16[8,512,512]{2,1,0:T(8,128...) while((s32[]{:T(128)}, f32[128,4,128]{0,2,1:T(8,128)}, ...), condition=%wide.region_27.28_spmd.clone, body=%wide.region_22.27_spmd.clone.sunk | while | flops 273627648 | bytes 11565616 | solution.py:56
  454.9 2.5 fusion.125
  466.6 2.5 fusion.125
  478.4 2.5 fusion.125
  490.1 2.5 fusion.125
  501.8 2.5 fusion.125
  513.6 2.5 fusion.125
  525.3 2.5 fusion.125
  533.4 165.6 %all-reduce.2.cloned.1.call-done = f32[512,1024]{1,0:T(8,128)} async-done(((f32[512,1024]{1,0:T(8,128)}), f32[512,1024]{1,0:T(8,128)}) %all-reduce.2.cloned.1.call-update) | async-done | bytes 2097168 | tf_op jit(solution)/shard_map/psum | solution.py:123
  698.9 3.2 copy.177
  (334 shorter events, 227.1 us)
Async XLA Ops:
  7.2 210.9 %copy-start = (bf16[512,1024]{1,0:T(8,128)(2,1)S(1)}, bf16[512,1024]{1,0:T(8,128)(2,1)}, u32[]{:S(2)}) copy-start(bf16[512,1024]{1,0:T(8,128)(2,1)} %param.21) | copy-start | bytes 3145732
  7.2 71.9 %all-gather.6.cloned.1.call-start = ((), (), s32[]{:S(2)}) async-start(), calls=%async_computation | async-start | bytes 4325376 | tf_op jit(solution)/shard_map/all_gather | solution.py:97
  7.9 139.5 %all-gather.8.cloned.1.call-start = ((), (), s32[]{:S(2)}) async-start(), calls=%async_computation.1 | async-start | bytes 4325376 | tf_op jit(solution)/shard_map/all_gather | solution.py:96
  8.7 293.7 %all-gather.10.cloned.1.call-start = ((), (), s32[]{:S(2)}) async-start(), calls=%async_computation.2 | async-start | bytes 2162688 | tf_op jit(solution)/shard_map/all_gather | solution.py:111
  9.4 427.7 %all-gather.12.cloned.1.call-start = ((), (), s32[]{:S(2)}) async-start(), calls=%async_computation.3 | async-start | bytes 4325376 | tf_op jit(solution)/shard_map/all_gather | solution.py:193
  10.0 427.1 %all-gather.14.cloned.1.call-start = ((), (), s32[]{:S(2)}) async-start(), calls=%async_computation.4 | async-start | bytes 4325376 | tf_op jit(solution)/shard_map/all_gather | solution.py:194
  153.9 64.1 %copy-start.4 = (bf16[128,1024]{1,0:T(8,128)(2,1)S(1)}, bf16[128,1024]{1,0:T(8,128)(2,1)}, u32[]{:S(2)}) copy-start(bf16[128,1024]{1,0:T(8,128)(2,1)} %param.23) | copy-start | bytes 786436
  153.9 64.2 %copy-start.6 = (bf16[128,512]{1,0:T(8,128)(2,1)S(1)}, bf16[128,512]{1,0:T(8,128)(2,1)}, u32[]{:S(2)}) copy-start(bf16[128,512]{1,0:T(8,128)(2,1)} %param.20) | copy-start | bytes 393220
  219.5 0.7 copy-start.2
  220.3 478.7 %all-reduce.2.cloned.1.call-start = ((), (), s32[]{:S(2)}) async-start(), calls=%async_computation.5 | async-start | bytes 4194304 | tf_op jit(solution)/shard_map/psum | solution.py:123
  305.1 130.2 %copy-start.3 = (bf16[128,512]{1,0:T(8,128)(2,1)S(1)}, bf16[128,512]{1,0:T(8,128)(2,1)}, u32[]{:S(2)}) copy-start(bf16[128,512]{1,0:T(8,128)(2,1)} %get-tuple-element.1178) | copy-start | bytes 393220
  305.1 130.2 %copy-start.5 = (bf16[128,1024]{1,0:T(8,128)(2,1)S(1)}, bf16[128,1024]{1,0:T(8,128)(2,1)}, u32[]{:S(2)}) copy-start(bf16[128,1024]{1,0:T(8,128)(2,1)} %param.23) | copy-start | bytes 786436
  434.6 2.5 copy-start.1
Sparse Core Ops, SparseCore 0:
  9.9 69.1 all-gather.5
  80.9 66.4 all-gather.7
  149.3 64.3 all-gather.9
  215.4 66.5 all-gather.11
  283.7 66.5 all-gather.13
  437.2 261.7 all-reduce.1
where the time goes:
time: 712 us; the launch traced here: 709 us
  waiting for transfers between devices  289 us (41%)
  local copies, waits for them, and re-layouts  217 us (30%)
  other arithmetic  101 us (14%)
  matrix products  86.5 us (12%)
  between operations  14.3 us (2%)
    psum x1, waiting for transfers between devices, body(): grad_out_weight = lax.psum(weight_local, ('dp', 'ctx'))  166 us
    gather x1, local copies, waits for them, and re-layouts, body(): scores = jnp.take_along_axis(all_scores, picked, axis=1)  129 us
    dynamic_slice x64, local copies, waits for them, and re-layouts, blockwise(): result, unused = lax.scan(advance, running, (stacked, offsets))  62.8 us
    all_gather x1, waiting for transfers between devices, body(): lax.all_gather(key, 'ctx', axis=0, tiled=True)  61.9 us
    all_gather x1, waiting for transfers between devices, body(): lax.all_gather(value, 'ctx', axis=0, tiled=True)  58.6 us
    unnamed x24, local copies, waits for them, and re-layouts  22.2 us
    dot_general x8, matrix products, key_step(): jnp.einsum('hqk,qhd->khd', grad_logits, query_piece, preferred_element_ty...  19.7 us
    dot_general x8, matrix products, query_step(): jnp.einsum('hqk,khd->qhd', grad_logits, key_piece, preferred_element_type...  19.6 us
  transfers between devices with their start and end apart: 6, of which 3 were waited for; matrix products, arithmetic and copies ran while one was open for 57% of the time, Pallas kernels for 0%

commit v1 on v0

--- a/solution.py
+++ b/solution.py
@@ -120,7 +120,7 @@
     weight_local = lax.dot_general(
         mixed, cotangent, (((0,), (0,)), ((), ())), preferred_element_type=jnp.float32
     )
-    grad_out_weight = lax.psum(weight_local, ("dp", "ctx"))
+    grad_out_weight = lax.psum(lax.psum(weight_local, "dp"), "ctx")
     grad_mixed = lax.dot_general(
         cotangent, out_weight, (((1,), (1,)), ((), ())), preferred_element_type=jnp.float32
     )

time: 712 us -> 701 us (0.985)
  waiting for transfers between devices: 289 us -> 277 us
    psum x1 -> x2, waiting for transfers between devices: 166 us -> 134 us  [body(): grad_out_weight = lax.psum(lax.psum(weight_local, 'dp'), 'ctx')]
    all_gather x1, waiting for transfers between devices: 0.02 us -> 14.4 us  [body(): lax.all_gather(grad_attended, 'ctx', axis=0, tiled=True)]
    unnamed x24 -> x32, local copies, waits for them, and re-layouts: 22.2 us -> 21.1 us
  transfers between devices with their start and end apart: 6 -> 7, of which waited for: 3 -> 4; matrix products, arithmetic and copies ran while one was open for 57% -> 57% of each run, Pallas kernels for 0% -> 0%
where the time goes in v1:
time: 701 us; the launch traced here: 696 us
  waiting for transfers between devices  277 us (40%)
  local copies, waits for them, and re-layouts  216 us (31%)
  other arithmetic  102 us (15%)
  matrix products  86.2 us (12%)
  between operations  14.4 us (2%)
    psum x2, waiting for transfers between devices, body(): grad_out_weight = lax.psum(lax.psum(weight_local, 'dp'), 'ctx')  134 us
    gather x1, local copies, waits for them, and re-layouts, body(): scores = jnp.take_along_axis(all_scores, picked, axis=1)  129 us
    all_gather x1, waiting for transfers between devices, body(): lax.all_gather(value, 'ctx', axis=0, tiled=True)  63.6 us
    dynamic_slice x64, local copies, waits for them, and re-layouts, blockwise(): result, unused = lax.scan(advance, running, (stacked, offsets))  62.6 us
    all_gather x1, waiting for transfers between devices, body(): lax.all_gather(key, 'ctx', axis=0, tiled=True)  61.9 us
    unnamed x32, local copies, waits for them, and re-layouts  21.1 us
    dot_general x8, matrix products, query_step(): jnp.einsum('hqk,khd->qhd', grad_logits, key_piece, preferred_element_type...  19.7 us
    dot_general x8, matrix products, key_step(): jnp.einsum('hqk,qhd->khd', grad_logits, query_piece, preferred_element_ty...  19.4 us
  transfers between devices with their start and end apart: 7, of which 4 were waited for; matrix products, arithmetic and copies ran while one was open for 57% of the time, Pallas kernels for 0%

profile of v1, /device:TPU:2, one launch (start us, length us, event | category | flops | bytes accessed | tf_op | source)
XLA Modules:
  0.0 695.7 jit_solution(9095168926770038452)
XLA Ops:
  15.5 63.6 %all-gather.6.cloned.1.call-done = bf16[4096,512]{1,0:T(8,128)(2,1)} async-done(((bf16[128,512]{1,0:T(8,128)(2,1)}), bf16[4096,512]{1,0:T(8,128)(2,1)}) %all-gather.6.cloned.1.call-update) | async-done | bytes 4194320 | tf_op jit(solution)/shard_map/all_gather | solution.py:97
  79.1 6.5 copy.119
  85.6 61.9 %all-gather.8.cloned.1.call-done = bf16[4096,512]{1,0:T(8,128)(2,1)} async-done(((bf16[128,512]{1,0:T(8,128)(2,1)}), bf16[4096,512]{1,0:T(8,128)(2,1)}) %all-gather.8.cloned.1.call-update) | async-done | bytes 4194320 | tf_op jit(solution)/shard_map/all_gather | solution.py:96
  147.4 6.5 copy.120
  153.9 64.1 %while.44 = (s32[]{:T(128)}, f32[128,4,128]{0,2,1:T(8,128)S(1)}, bf16[8,512,512]{1,2,0:T(8,128)(2,1)}, bf16[8,512,512]{1,2,0:T(8,128)(2,1)}, bf16[128,4,128]{2,0...) while((s32[]{:T(128)}, f32[128,4,128]{0,2,1:T(8,128)S(1)}, ...), condition=%wide.region_11.12_spmd.clone, body=%wide.region_6.11_spmd.clone.sunk | while | flops 136657424 | bytes 4356639 | solution.py:56
  225.7 80.6 %while.45 = (s32[]{:T(128)}, f32[128,4,128]{0,2,1:T(8,128)}, bf16[8,512,512]{1,2,0:T(8,128)(2,1)}, bf16[8,512,512]{1,2,0:T(8,128)(2,1)}, bf16[128,4,128]{2,0,1:T...) while((s32[]{:T(128)}, f32[128,4,128]{0,2,1:T(8,128)}, ...), condition=%wide.region_21.22_spmd.clone, body=%wide.region_16.21_spmd.clone.sunk | while | flops 204814864 | bytes 7109159 | solution.py:56
  243.3 2.5 fusion.118
  253.4 2.5 fusion.118
  263.5 2.5 fusion.118
  273.6 2.5 fusion.118
  283.6 2.5 fusion.118
  293.7 2.5 fusion.118
  303.8 2.5 fusion.118
  308.0 2.7 fusion.53
  310.7 129.5 %gather_fusion = f32[16384]{0:T(1024)S(1)} fusion(f32[128,1024]{1,0:T(8,128)S(1)} %fusion.53, s32[16384]{0:T(1024)S(1)} %fusion.59), kind=kCustom, calls=%fused_computation | custom fusion | bytes 262144 | tf_op jit(solution)/shard_map/jit(take_along_axis)/gather | solution.py:119
  440.9 14.4 %all-gather.14.cloned.1.call-done = bf16[4096,512]{1,0:T(8,128)(2,1)} async-done(((bf16[128,512]{1,0:T(8,128)(2,1)}), bf16[4096,512]{1,0:T(8,128)(2,1)}) %all-gather.14.cloned.1.call-update) | async-done | bytes 4194320 | tf_op jit(solution)/shard_map/all_gather | solution.py:194
  455.3 92.7 %while.46 = (s32[]{:T(128)}, f32[128,4,128]{0,2,1:T(8,128)}, f32[128,4,128]{0,2,1:T(8,128)}, bf16[8,512,512]{2,1,0:T(8,128)(2,1)}, bf16[8,512,512]{2,1,0:T(8,128...) while((s32[]{:T(128)}, f32[128,4,128]{0,2,1:T(8,128)}, ...), condition=%wide.region_27.28_spmd.clone, body=%wide.region_22.27_spmd.clone.sunk | while | flops 273627648 | bytes 11565616 | solution.py:56
  473.1 2.4 fusion.125
  484.8 2.4 fusion.125
  496.6 2.4 fusion.125
  508.3 2.4 fusion.125
  543.4 2.4 fusion.125
  551.5 134.1 %all-reduce.5.cloned.1.call-done = f32[512,1024]{1,0:T(8,128)} async-done(((f32[512,1024]{1,0:T(8,128)}), f32[512,1024]{1,0:T(8,128)}) %all-reduce.5.cloned.1.call-update) | async-done | bytes 2097168 | tf_op jit(solution)/shard_map/psum | solution.py:123
  685.7 3.2 copy.178
  (345 shorter events, 228.6 us)
Async XLA Ops:
  7.2 211.2 %copy-start = (bf16[512,1024]{1,0:T(8,128)(2,1)S(1)}, bf16[512,1024]{1,0:T(8,128)(2,1)}, u32[]{:S(2)}) copy-start(bf16[512,1024]{1,0:T(8,128)(2,1)} %param.21) | copy-start | bytes 3145732
  7.2 71.9 %all-gather.6.cloned.1.call-start = ((), (), s32[]{:S(2)}) async-start(), calls=%async_computation | async-start | bytes 4325376 | tf_op jit(solution)/shard_map/all_gather | solution.py:97
  7.9 139.5 %all-gather.8.cloned.1.call-start = ((), (), s32[]{:S(2)}) async-start(), calls=%async_computation.1 | async-start | bytes 4325376 | tf_op jit(solution)/shard_map/all_gather | solution.py:96
  8.7 299.4 %all-gather.10.cloned.1.call-start = ((), (), s32[]{:S(2)}) async-start(), calls=%async_computation.2 | async-start | bytes 2162688 | tf_op jit(solution)/shard_map/all_gather | solution.py:111
  9.4 431.5 %all-reduce.3.cloned.1.call-start = ((), (), s32[]{:S(2)}) async-start(), calls=%async_computation.5 | async-start | bytes 4194304 | tf_op jit(solution)/shard_map/psum | solution.py:123
  153.9 64.4 %copy-start.4 = (bf16[128,1024]{1,0:T(8,128)(2,1)S(1)}, bf16[128,1024]{1,0:T(8,128)(2,1)}, u32[]{:S(2)}) copy-start(bf16[128,1024]{1,0:T(8,128)(2,1)} %param.23) | copy-start | bytes 786436
  153.9 64.4 %copy-start.9 = (bf16[128,512]{1,0:T(8,128)(2,1)S(1)}, bf16[128,512]{1,0:T(8,128)(2,1)}, u32[]{:S(2)}) copy-start(bf16[128,512]{1,0:T(8,128)(2,1)} %param.20) | copy-start | bytes 393220
  218.1 4.8 copy-start.7
  218.2 4.8 copy-start.8
  218.4 6.4 copy-start.10
  219.8 0.7 copy-start.3
  219.8 5.8 copy-start.2
  222.2 218.7 %all-gather.12.cloned.1.call-start = ((), (), s32[]{:S(2)}) async-start(), calls=%async_computation.3 | async-start | bytes 4325376 | tf_op jit(solution)/shard_map/all_gather | solution.py:193
  222.8 232.5 %all-gather.14.cloned.1.call-start = ((), (), s32[]{:S(2)}) async-start(), calls=%async_computation.4 | async-start | bytes 4325376 | tf_op jit(solution)/shard_map/all_gather | solution.py:194
  224.9 0.8 copy-start.5
  225.6 460.0 %all-reduce.5.cloned.1.call-start = ((), (), s32[]{:S(2)}) async-start(), calls=%async_computation.6 | async-start | bytes 4194304 | tf_op jit(solution)/shard_map/psum | solution.py:123
  310.7 129.5 %copy-start.6 = (s32[128,128]{1,0:T(8,128)S(1)}, s32[128,128]{1,0:T(8,128)}, u32[]{:S(2)}) copy-start(s32[128,128]{1,0:T(8,128)} %copy-done.5) | copy-start | bytes 196612
  310.7 144.6 %copy-start.1 = (bf16[128,4,128]{2,0,1:T(8,128)(2,1)S(1)}, bf16[128,4,128]{2,0,1:T(8,128)(2,1)}, u32[]{:S(2)}) copy-start(bf16[128,4,128]{2,0,1:T(8,128)(2,1)} %copy.133) | copy-start | bytes 393220
Sparse Core Ops, SparseCore 0:
  9.9 69.1 all-gather.5
  80.9 66.4 all-gather.7
  149.3 64.4 all-gather.9
  222.4 96.9 all-reduce.2
  321.0 66.2 all-gather.11
  389.0 66.2 all-gather.13
  457.9 227.6 all-reduce.4
